TPU v7x, 32 devices: a whole 2x2x4 slice. The times are simulated.
32 devices in a mesh: sect: 2 (over x), slab: 8 (over z, y), energy: 2 (over core).
Axes of the slice: x: 2, y: 2, z: 4, core: 2. Of those that a mesh axis runs over, the one named last changes fastest.
Arguments:
- source: bfloat16 [4, 512, 128], P(('energy', 'sect'), 'slab'), parts along dimension 0, may hold values from -6 to 6
- forward_mult: bfloat16 [4, 2, 512, 512], P(('energy', 'sect'), None, 'slab'), parts along dimension 0, may hold values from -0.1875 to 0.1875
- schur_inverse: bfloat16 [4, 2, 512, 512], P(('energy', 'sect'), None, 'slab'), parts along dimension 0, may hold values from -0.09375 to 0.09375
- upper_mult: bfloat16 [4, 2, 512, 512], P(('energy', 'sect'), None, 'slab'), parts along dimension 0, may hold values from -0.125 to 0.125
Outputs:
- wave: bfloat16 [4, 512, 128], P(('energy', 'sect'), 'slab'), parts along dimension 0
There are 2 independent parts, one for each index of `energy`. A program takes and returns all parts, laid end to end along the dimension named above; each array names one. Nothing has to cross between parts.
All inputs are finite; a program needn't handle non-finite values.
Results may differ from a plain program's by a relative error of at most 0.012.
Values may be sent and summed in bfloat16 or wider, within the bound.
No kernel may reach another device: no remote copies, remote signals or barrier semaphores. Data moves between devices by JAX's collectives and lax.ppermute only.
A program may use at most 64 MiB of HBM per device.

v0:
```python
import jax
import jax.numpy as jnp
from jax import lax
from jax.sharding import PartitionSpec as P


def from_behind(block, axis, distance):
    devices = range(lax.axis_size(axis))
    route = [(i - distance, i) for i in devices if i - distance in devices]
    return lax.ppermute(block, axis, route)


def complex_apply(matrix, vector):
    half_cols = vector.shape[1] // 2
    real_part = jnp.dot(matrix[0], vector, preferred_element_type=jnp.float32)
    imag_part = jnp.dot(matrix[1], vector, preferred_element_type=jnp.float32)
    return jnp.concatenate(
        [
            real_part[:, :half_cols] - imag_part[:, half_cols:],
            real_part[:, half_cols:] + imag_part[:, :half_cols],
        ],
        axis=1,
    )


def fold_rows(matrix, rows_in):
    return complex_apply(matrix, rows_in)


def per_device(source, forward_mult, schur_inverse, upper_mult):
    local_src = source[0]
    forward_local = forward_mult[0]
    inverse_local = schur_inverse[0]
    upper_local = upper_mult[0]
    sections = lax.axis_size("sect")
    src_float = local_src.astype(jnp.float32)

    def forward_segment(segment_no, current):
        inflow = from_behind(current, "sect", 1)
        summed = fold_rows(forward_local, lax.all_gather(inflow, "slab", axis=0, tiled=True))
        return (src_float + summed).astype(jnp.bfloat16)

    forward_rows = lax.fori_loop(0, sections, forward_segment, local_src)
    scaled = fold_rows(inverse_local, lax.all_gather(forward_rows, "slab", axis=0, tiled=True))

    def backward_segment(segment_no, current):
        outflow = from_behind(current, "sect", -1)
        summed = fold_rows(upper_local, lax.all_gather(outflow, "slab", axis=0, tiled=True))
        return (scaled - summed).astype(jnp.bfloat16)

    wave_rows = lax.fori_loop(0, sections, backward_segment, scaled.astype(jnp.bfloat16))
    return wave_rows[None]


def solution(mesh):
    in_specs = (
        P(("energy", "sect"), "slab", None),
        P(("energy", "sect"), None, "slab", None),
        P(("energy", "sect"), None, "slab", None),
        P(("energy", "sect"), None, "slab", None),
    )
    out_specs = P(("energy", "sect"), "slab", None)
    return jax.shard_map(
        per_device, mesh=mesh, in_specs=in_specs, out_specs=out_specs, check_vma=False
    )
```

profile of v0, /device:TPU:0, one launch (start us, length us, event | category | flops | bytes accessed | tf_op | source)
XLA Modules:
  0.0 181.1 jit_solution(12969878950898552480)
XLA Ops:
  0.0 0.7 copy.19
  0.7 74.7 %while.20 = (s32[]{:T(128)}, bf16[64,128]{1,0:T(8,128)(2,1)S(1)}, bf16[2,64,512]{2,1,0:T(8,128)(2,1)}, f32[64,128]{1,0:T(8,128)S(1)}, s32[]{:T(128)}) while((s32[]{:T(128)}, bf16[64,128]{1,0:T(8,128)(2,1)S(1)}, bf16[2,64,512]{2,1,0:T(8,128)(2,1)}, f32[64,128]{1,0:T(8,128)S(1)}, s32[]{:T(128)}) %tuple.47), condition=%wide.region_1.0_spmd, body=%wide.region_0.0_spmd.sunk | while | flops 16809984 | bytes 1376385 | solution.py:43
  0.7 0.0 copy-start
  0.7 5.0 %collective-permute-start = (bf16[64,128]{1,0:T(8,128)(2,1)S(1)}, bf16[64,128]{1,0:T(8,128)(2,1)S(1)}, u32[]{:S(2)}, u32[]{:S(2)}) collective-permute-start(bf16[64,128]{1,0:T(8,128)(2,1)S(1)} %get-tuple-element.139), channel_id=1, source_target_pairs={{0,16},{1,17},{2,18},{3,19},{4,20},{5,21},{6,22},{7,23},{8,24},{9,... | collective-permute-start | bytes 49160 | tf_op jit(solution)/shard_map/while/body/eval_jaxpr/ppermute | solution.py:10
  5.7 1.4 collective-permute-done
  7.2 30.8 %all_gather.12 = bf16[512,128]{1,0:T(8,128)(2,1)S(1)} all-gather(bf16[64,128]{1,0:T(8,128)(2,1)S(1)} %collective-permute-done), channel_id=1, replica_groups=mesh['sect'=2,'slab'=8,'energy'=2] {'slab'}, dimensions={0}, use_global_device_ids=true | all-gather | bytes 147456 | tf_op jit(solution)/shard_map/while/body/eval_jaxpr/all_gather | solution.py:40
  38.0 0.0 copy-done
  38.0 0.2 fusion.44
  38.2 0.2 fusion.43
  38.3 0.1 slice_subtract_fusion.5
  38.4 0.1 fusion.45
  38.5 0.0 copy-start
  38.5 4.4 %collective-permute-start = (bf16[64,128]{1,0:T(8,128)(2,1)S(1)}, bf16[64,128]{1,0:T(8,128)(2,1)S(1)}, u32[]{:S(2)}, u32[]{:S(2)}) collective-permute-start(bf16[64,128]{1,0:T(8,128)(2,1)S(1)} %get-tuple-element.139), channel_id=1, source_target_pairs={{0,16},{1,17},{2,18},{3,19},{4,20},{5,21},{6,22},{7,23},{8,24},{9,... | collective-permute-start | bytes 49160 | tf_op jit(solution)/shard_map/while/body/eval_jaxpr/ppermute | solution.py:10
  42.9 1.4 collective-permute-done
  44.3 30.6 %all_gather.12 = bf16[512,128]{1,0:T(8,128)(2,1)S(1)} all-gather(bf16[64,128]{1,0:T(8,128)(2,1)S(1)} %collective-permute-done), channel_id=1, replica_groups=mesh['sect'=2,'slab'=8,'energy'=2] {'slab'}, dimensions={0}, use_global_device_ids=true | all-gather | bytes 147456 | tf_op jit(solution)/shard_map/while/body/eval_jaxpr/all_gather | solution.py:40
  74.9 0.0 copy-done
  74.9 0.2 fusion.44
  75.1 0.2 fusion.43
  75.2 0.1 slice_subtract_fusion.5
  75.3 0.1 fusion.45
  75.4 0.0 copy-start.2
  75.4 30.7 %all_gather.9 = bf16[512,128]{1,0:T(8,128)(2,1)S(1)} all-gather(bf16[64,128]{1,0:T(8,128)(2,1)S(1)} %get-tuple-element.49), channel_id=1, replica_groups=mesh['sect'=2,'slab'=8,'energy'=2] {'slab'}, dimensions={0}, use_global_device_ids=true | all-gather | bytes 147456 | tf_op jit(solution)/shard_map/all_gather | solution.py:44
  106.1 0.0 copy-done.2
  106.1 0.2 convolution_bitcast_fusion.1
  106.2 0.2 convolution_bitcast_fusion
  106.4 0.0 copy-start.1
  106.4 0.1 slice_subtract_fusion.2
  106.5 0.1 fusion.18
  106.6 0.7 copy-done.1
  107.3 73.2 %while.21 = (s32[]{:T(128)}, bf16[64,128]{1,0:T(8,128)(2,1)S(1)}, bf16[2,64,512]{2,1,0:T(8,128)(2,1)S(1)}, f32[64,128]{1,0:T(8,128)S(1)}, s32[]{:T(128)}) while((s32[]{:T(128)}, bf16[64,128]{1,0:T(8,128)(2,1)S(1)}, bf16[2,64,512]{2,1,0:T(8,128)(2,1)S(1)}, f32[64,128]{1,0:T(8,128)S(1)}, s32[]{:T(128)}) %tuple.46), condition=%wide.region_3.0_spmd, body=%wide.region_2.0_spmd.sunk | while | flops 16809984 | bytes 852069 | solution.py:51
  107.3 1.3 collective-permute-start.1
  108.6 4.3 %collective-permute-done.1 = bf16[64,128]{1,0:T(8,128)(2,1)S(1)} collective-permute-done((bf16[64,128]{1,0:T(8,128)(2,1)S(1)}, bf16[64,128]{1,0:T(8,128)(2,1)S(1)}, u32[]{:S(2)}, u32[]{:S(2)}) %collective-permute-start.1) | collective-permute-done | bytes 16416 | tf_op jit(solution)/shard_map/while/body/eval_jaxpr/ppermute | solution.py:10
  112.9 30.5 %all_gather.13 = bf16[512,128]{1,0:T(8,128)(2,1)S(1)} all-gather(bf16[64,128]{1,0:T(8,128)(2,1)S(1)} %collective-permute-done.1), channel_id=1, replica_groups=mesh['sect'=2,'slab'=8,'energy'=2] {'slab'}, dimensions={0}, use_global_device_ids=true | all-gather | bytes 147456 | tf_op jit(solution)/shard_map/while/body/eval_jaxpr/all_gather | solution.py:48
  143.4 0.2 fusion.51
  143.6 0.2 fusion.50
  143.7 0.1 slice_subtract_fusion.6
  143.8 0.1 fusion.52
  143.9 1.3 collective-permute-start.1
  145.2 4.3 %collective-permute-done.1 = bf16[64,128]{1,0:T(8,128)(2,1)S(1)} collective-permute-done((bf16[64,128]{1,0:T(8,128)(2,1)S(1)}, bf16[64,128]{1,0:T(8,128)(2,1)S(1)}, u32[]{:S(2)}, u32[]{:S(2)}) %collective-permute-start.1) | collective-permute-done | bytes 16416 | tf_op jit(solution)/shard_map/while/body/eval_jaxpr/ppermute | solution.py:10
  149.5 30.5 %all_gather.13 = bf16[512,128]{1,0:T(8,128)(2,1)S(1)} all-gather(bf16[64,128]{1,0:T(8,128)(2,1)S(1)} %collective-permute-done.1), channel_id=1, replica_groups=mesh['sect'=2,'slab'=8,'energy'=2] {'slab'}, dimensions={0}, use_global_device_ids=true | all-gather | bytes 147456 | tf_op jit(solution)/shard_map/while/body/eval_jaxpr/all_gather | solution.py:48
  180.1 0.2 fusion.51
  180.2 0.2 fusion.50
  180.4 0.1 slice_subtract_fusion.6
  180.5 0.1 fusion.52
  180.5 0.0 copy-start.3
  180.5 0.6 copy-done.3
  (1 shorter events, 0.0 us)
Async XLA Ops:
  0.7 37.3 %copy-start = (bf16[2,64,512]{2,1,0:T(8,128)(2,1)S(1)}, bf16[2,64,512]{2,1,0:T(8,128)(2,1)}, u32[]{:S(2)}) copy-start(bf16[2,64,512]{2,1,0:T(8,128)(2,1)} %get-tuple-element.145) | copy-start | bytes 393220 | tf_op jit(solution)/shard_map/while
  0.7 6.4 %collective-permute-start = (bf16[64,128]{1,0:T(8,128)(2,1)S(1)}, bf16[64,128]{1,0:T(8,128)(2,1)S(1)}, u32[]{:S(2)}, u32[]{:S(2)}) collective-permute-start(bf16[64,128]{1,0:T(8,128)(2,1)S(1)} %get-tuple-element.139), channel_id=1, source_target_pairs={{0,16},{1,17},{2,18},{3,19},{4,20},{5,21},{6,22},{7,23},{8,24},{9,... | collective-permute-start | bytes 49160 | tf_op jit(solution)/shard_map/while/body/eval_jaxpr/ppermute | solution.py:10
  38.5 36.4 %copy-start = (bf16[2,64,512]{2,1,0:T(8,128)(2,1)S(1)}, bf16[2,64,512]{2,1,0:T(8,128)(2,1)}, u32[]{:S(2)}) copy-start(bf16[2,64,512]{2,1,0:T(8,128)(2,1)} %get-tuple-element.145) | copy-start | bytes 393220 | tf_op jit(solution)/shard_map/while
  38.5 5.8 %collective-permute-start = (bf16[64,128]{1,0:T(8,128)(2,1)S(1)}, bf16[64,128]{1,0:T(8,128)(2,1)S(1)}, u32[]{:S(2)}, u32[]{:S(2)}) collective-permute-start(bf16[64,128]{1,0:T(8,128)(2,1)S(1)} %get-tuple-element.139), channel_id=1, source_target_pairs={{0,16},{1,17},{2,18},{3,19},{4,20},{5,21},{6,22},{7,23},{8,24},{9,... | collective-permute-start | bytes 49160 | tf_op jit(solution)/shard_map/while/body/eval_jaxpr/ppermute | solution.py:10
  75.4 30.7 %copy-start.2 = (bf16[1,2,64,512]{3,2,1,0:T(8,128)(2,1)S(1)}, bf16[1,2,64,512]{3,2,1,0:T(8,128)(2,1)}, u32[]{:S(2)}) copy-start(bf16[1,2,64,512]{3,2,1,0:T(8,128)(2,1)} %param.10) | copy-start | bytes 393220
  106.4 0.9 copy-start.1
  107.3 5.6 %collective-permute-start.1 = (bf16[64,128]{1,0:T(8,128)(2,1)S(1)}, bf16[64,128]{1,0:T(8,128)(2,1)S(1)}, u32[]{:S(2)}, u32[]{:S(2)}) collective-permute-start(bf16[64,128]{1,0:T(8,128)(2,1)S(1)} %get-tuple-element.154), channel_id=1, source_target_pairs={{16,0},{17,1},{18,2},{19,3},{20,4},{21,5},{22,6},{23,7},{24,8},{25... | collective-permute-start | bytes 49160 | tf_op jit(solution)/shard_map/while/body/eval_jaxpr/ppermute | solution.py:10
  143.9 5.6 %collective-permute-start.1 = (bf16[64,128]{1,0:T(8,128)(2,1)S(1)}, bf16[64,128]{1,0:T(8,128)(2,1)S(1)}, u32[]{:S(2)}, u32[]{:S(2)}) collective-permute-start(bf16[64,128]{1,0:T(8,128)(2,1)S(1)} %get-tuple-element.154), channel_id=1, source_target_pairs={{16,0},{17,1},{18,2},{19,3},{20,4},{21,5},{22,6},{23,7},{24,8},{25... | collective-permute-start | bytes 49160 | tf_op jit(solution)/shard_map/while/body/eval_jaxpr/ppermute | solution.py:10
  180.5 0.6 copy-start.3
where the time goes:
time: 181 us
  blocking collectives  153 us (85%)
  starting transfers between devices  12 us (7%)
  waiting for transfers between devices  11.5 us (6%)
  local copies, waits for them, and re-layouts  2.07 us (1%)
    all_gather x2, blocking collectives, forward_segment(): lax.all_gather(inflow, 'slab', axis=0, tiled=True)  61.4 us
    all_gather x2, blocking collectives, backward_segment(): lax.all_gather(outflow, 'slab', axis=0, tiled=True)  61 us
    all_gather x1, blocking collectives, per_device(): lax.all_gather(forward_rows, 'slab', axis=0, tiled=True)  30.7 us
    ppermute x4, starting transfers between devices, from_behind(): return lax.ppermute(block, axis, route)  12 us
    ppermute x4, waiting for transfers between devices, from_behind(): return lax.ppermute(block, axis, route)  11.5 us
  transfers between devices with their start and end apart: 4, of which 4 were waited for; matrix products, arithmetic and copies ran while one was open for 0% of the time, Pallas kernels for 0%

commit v1 on v0

--- a/solution.py
+++ b/solution.py
@@ -2,6 +2,29 @@
 import jax.numpy as jnp
 from jax import lax
 from jax.sharding import PartitionSpec as P
+
+
+def laid_out(blocks, dim):
+    shape = list(blocks.shape[1:])
+    shape[dim] *= blocks.shape[0]
+    return jnp.moveaxis(blocks, 0, dim).reshape(shape)
+
+
+def doubled(shard, axis):
+    size, index = (lax.axis_size(axis), lax.axis_index(axis))
+    blocks, apart = (shard[None], 1)
+    while apart < size:
+        received = lax.ppermute(blocks, axis, [(i, i ^ apart) for i in range(size)])
+        low = index & apart == 0
+        blocks = jnp.concatenate(
+            [jnp.where(low, blocks, received), jnp.where(low, received, blocks)]
+        )
+        apart *= 2
+    return blocks
+
+
+def gather_by_bits(shard, axis, dim):
+    return laid_out(doubled(shard, axis), dim)
 
 
 def from_behind(block, axis, distance):
@@ -41,7 +64,7 @@
         return (src_float + summed).astype(jnp.bfloat16)
 
     forward_rows = lax.fori_loop(0, sections, forward_segment, local_src)
-    scaled = fold_rows(inverse_local, lax.all_gather(forward_rows, "slab", axis=0, tiled=True))
+    scaled = fold_rows(inverse_local, gather_by_bits(forward_rows, "slab", 0))
 
     def backward_segment(segment_no, current):
         outflow = from_behind(current, "sect", -1)

time: 181 us -> 165 us (0.912)
  blocking collectives: 153 us -> 122 us
  waiting for transfers between devices: 11.5 us -> 22 us
  starting transfers between devices: 12 us -> 14.9 us
    all_gather x1 -> x0, blocking collectives: 30.7 us -> none  [per_device(): lax.all_gather(forward_rows, 'slab', axis=0, tiled=True)]
    ppermute x0 -> x3, waiting for transfers between devices: none -> 10.5 us  [doubled(): received = lax.ppermute(blocks, axis, [(i, i ^ apart) for i in range(size)])]
    ppermute x0 -> x3, starting transfers between devices: none -> 2.97 us  [doubled(): received = lax.ppermute(blocks, axis, [(i, i ^ apart) for i in range(size)])]
  transfers between devices with their start and end apart: 4 -> 7, of which waited for: 4 -> 7; matrix products, arithmetic and copies ran while one was open for 0% -> 0% of each run, Pallas kernels for 0% -> 0%
where the time goes in v1:
time: 165 us
  blocking collectives  122 us (74%)
  waiting for transfers between devices  22 us (13%)
  starting transfers between devices  14.9 us (9%)
  local copies, waits for them, and re-layouts  2.94 us (2%)
    all_gather x2, blocking collectives, forward_segment(): lax.all_gather(inflow, 'slab', axis=0, tiled=True)  61.4 us
    all_gather x2, blocking collectives, backward_segment(): lax.all_gather(outflow, 'slab', axis=0, tiled=True)  61 us
    ppermute x4, starting transfers between devices, from_behind(): return lax.ppermute(block, axis, route)  12 us
    ppermute x4, waiting for transfers between devices, from_behind(): return lax.ppermute(block, axis, route)  11.5 us
    ppermute x3, waiting for transfers between devices, doubled(): received = lax.ppermute(blocks, axis, [(i, i ^ apart) for i in range(size)])  10.5 us
  transfers between devices with their start and end apart: 7, of which 7 were waited for; matrix products, arithmetic and copies ran while one was open for 0% of the time, Pallas kernels for 0%

profile of v1, /device:TPU:0, one launch (start us, length us, event | category | flops | bytes accessed | tf_op | source)
XLA Modules:
  0.0 164.9 jit_solution(6343920039253333578)
XLA Ops:
  0.0 0.7 copy.19
  0.7 74.6 %while.20 = (s32[]{:T(128)}, bf16[64,128]{1,0:T(8,128)(2,1)S(1)}, bf16[2,64,512]{2,1,0:T(8,128)(2,1)}, f32[64,128]{1,0:T(8,128)S(1)}, s32[]{:T(128)}) while((s32[]{:T(128)}, bf16[64,128]{1,0:T(8,128)(2,1)S(1)}, bf16[2,64,512]{2,1,0:T(8,128)(2,1)}, f32[64,128]{1,0:T(8,128)S(1)}, s32[]{:T(128)}) %tuple.50), condition=%wide.region_1.0_spmd, body=%wide.region_0.0_spmd.sunk | while | flops 16809984 | bytes 1376385 | solution.py:66
  0.7 5.0 %collective-permute-start = (bf16[64,128]{1,0:T(8,128)(2,1)S(1)}, bf16[64,128]{1,0:T(8,128)(2,1)S(1)}, u32[]{:S(2)}, u32[]{:S(2)}) collective-permute-start(bf16[64,128]{1,0:T(8,128)(2,1)S(1)} %get-tuple-element.145), channel_id=1, source_target_pairs={{0,16},{1,17},{2,18},{3,19},{4,20},{5,21},{6,22},{7,23},{8,24},{9,... | collective-permute-start | bytes 49160 | tf_op jit(solution)/shard_map/while/body/eval_jaxpr/ppermute | solution.py:33
  5.7 1.4 collective-permute-done
  7.2 30.8 %all_gather.8 = bf16[512,128]{1,0:T(8,128)(2,1)S(1)} all-gather(bf16[64,128]{1,0:T(8,128)(2,1)S(1)} %collective-permute-done), channel_id=1, replica_groups=mesh['sect'=2,'slab'=8,'energy'=2] {'slab'}, dimensions={0}, use_global_device_ids=true | all-gather | bytes 147456 | tf_op jit(solution)/shard_map/while/body/eval_jaxpr/all_gather | solution.py:63
  38.0 0.0 copy-done
  38.0 0.2 fusion.44
  38.2 0.2 fusion.43
  38.3 0.1 slice_subtract_fusion.5
  38.4 0.1 fusion.45
  38.5 4.4 %collective-permute-start = (bf16[64,128]{1,0:T(8,128)(2,1)S(1)}, bf16[64,128]{1,0:T(8,128)(2,1)S(1)}, u32[]{:S(2)}, u32[]{:S(2)}) collective-permute-start(bf16[64,128]{1,0:T(8,128)(2,1)S(1)} %get-tuple-element.145), channel_id=1, source_target_pairs={{0,16},{1,17},{2,18},{3,19},{4,20},{5,21},{6,22},{7,23},{8,24},{9,... | collective-permute-start | bytes 49160 | tf_op jit(solution)/shard_map/while/body/eval_jaxpr/ppermute | solution.py:33
  42.9 1.4 collective-permute-done
  44.3 30.5 %all_gather.8 = bf16[512,128]{1,0:T(8,128)(2,1)S(1)} all-gather(bf16[64,128]{1,0:T(8,128)(2,1)S(1)} %collective-permute-done), channel_id=1, replica_groups=mesh['sect'=2,'slab'=8,'energy'=2] {'slab'}, dimensions={0}, use_global_device_ids=true | all-gather | bytes 147456 | tf_op jit(solution)/shard_map/while/body/eval_jaxpr/all_gather | solution.py:63
  74.9 0.0 copy-done
  74.9 0.2 fusion.44
  75.0 0.2 fusion.43
  75.2 0.1 slice_subtract_fusion.5
  75.3 0.1 fusion.45
  75.4 1.5 collective-permute-start.2
  76.9 2.3 %collective-permute-done.2 = bf16[1,64,128]{2,1,0:T(8,128)(2,1)S(1)} collective-permute-done((bf16[1,64,128]{2,1,0:T(8,128)(2,1)S(1)}, bf16[1,64,128]{2,1,0:T(8,128)(2,1)S(1)}, u32[]{:S(2)}, u32[]{:S(2)}) %collective-permute-start.2) | collective-permute-done | bytes 16416 | tf_op jit(solution)/shard_map/ppermute | solution.py:17
  79.1 0.1 collective-permute-start.3
  79.2 3.9 %collective-permute-done.3 = bf16[2,64,128]{2,1,0:T(8,128)(2,1)S(1)} collective-permute-done((bf16[2,64,128]{2,1,0:T(8,128)(2,1)S(1)}, bf16[2,64,128]{2,1,0:T(8,128)(2,1)S(1)}, u32[]{:S(2)}, u32[]{:S(2)}) %collective-permute-start.3) | collective-permute-done | bytes 32800 | tf_op jit(solution)/shard_map/ppermute | solution.py:17
  83.2 1.4 collective-permute-start.4
  84.6 4.3 %collective-permute-done.4 = bf16[4,64,128]{2,1,0:T(8,128)(2,1)S(1)} collective-permute-done((bf16[4,64,128]{2,1,0:T(8,128)(2,1)S(1)}, bf16[4,64,128]{2,1,0:T(8,128)(2,1)S(1)}, u32[]{:S(2)}, u32[]{:S(2)}) %collective-permute-start.4) | collective-permute-done | bytes 65568 | tf_op jit(solution)/shard_map/ppermute | solution.py:17
  88.9 0.0 copy-start.2
  88.9 0.9 copy-done.2
  89.8 0.2 convolution_bitcast_fusion.1
  90.0 0.2 convolution_bitcast_fusion
  90.1 0.0 copy-start.1
  90.1 0.1 slice_subtract_fusion.2
  90.2 0.1 fusion.18
  90.3 0.7 copy-done.1
  91.0 73.3 %while.21 = (s32[]{:T(128)}, bf16[64,128]{1,0:T(8,128)(2,1)S(1)}, bf16[2,64,512]{2,1,0:T(8,128)(2,1)S(1)}, f32[64,128]{1,0:T(8,128)S(1)}, s32[]{:T(128)}) while((s32[]{:T(128)}, bf16[64,128]{1,0:T(8,128)(2,1)S(1)}, bf16[2,64,512]{2,1,0:T(8,128)(2,1)S(1)}, f32[64,128]{1,0:T(8,128)S(1)}, s32[]{:T(128)}) %tuple.49), condition=%wide.region_3.4_spmd, body=%wide.region_2.3_spmd.sunk | while | flops 16809984 | bytes 852069 | solution.py:74
  91.0 1.3 collective-permute-start.1
  92.3 4.3 %collective-permute-done.1 = bf16[64,128]{1,0:T(8,128)(2,1)S(1)} collective-permute-done((bf16[64,128]{1,0:T(8,128)(2,1)S(1)}, bf16[64,128]{1,0:T(8,128)(2,1)S(1)}, u32[]{:S(2)}, u32[]{:S(2)}) %collective-permute-start.1) | collective-permute-done | bytes 16416 | tf_op jit(solution)/shard_map/while/body/eval_jaxpr/ppermute | solution.py:33
  96.6 30.5 %all_gather.9 = bf16[512,128]{1,0:T(8,128)(2,1)S(1)} all-gather(bf16[64,128]{1,0:T(8,128)(2,1)S(1)} %collective-permute-done.1), channel_id=1, replica_groups=mesh['sect'=2,'slab'=8,'energy'=2] {'slab'}, dimensions={0}, use_global_device_ids=true | all-gather | bytes 147456 | tf_op jit(solution)/shard_map/while/body/eval_jaxpr/all_gather | solution.py:71
  127.2 0.2 fusion.51
  127.3 0.2 fusion.50
  127.5 0.1 slice_subtract_fusion.6
  127.6 0.1 fusion.52
  127.7 1.3 collective-permute-start.1
  129.0 4.3 %collective-permute-done.1 = bf16[64,128]{1,0:T(8,128)(2,1)S(1)} collective-permute-done((bf16[64,128]{1,0:T(8,128)(2,1)S(1)}, bf16[64,128]{1,0:T(8,128)(2,1)S(1)}, u32[]{:S(2)}, u32[]{:S(2)}) %collective-permute-start.1) | collective-permute-done | bytes 16416 | tf_op jit(solution)/shard_map/while/body/eval_jaxpr/ppermute | solution.py:33
  133.3 30.5 %all_gather.9 = bf16[512,128]{1,0:T(8,128)(2,1)S(1)} all-gather(bf16[64,128]{1,0:T(8,128)(2,1)S(1)} %collective-permute-done.1), channel_id=1, replica_groups=mesh['sect'=2,'slab'=8,'energy'=2] {'slab'}, dimensions={0}, use_global_device_ids=true | all-gather | bytes 147456 | tf_op jit(solution)/shard_map/while/body/eval_jaxpr/all_gather | solution.py:71
  163.8 0.2 fusion.51
  164.0 0.2 fusion.50
  164.1 0.1 slice_subtract_fusion.6
  164.2 0.1 fusion.52
  164.3 0.6 copy-done.3
  (10 shorter events, 0.1 us)
Async XLA Ops:
  0.7 37.3 %copy-start = (bf16[2,64,512]{2,1,0:T(8,128)(2,1)S(1)}, bf16[2,64,512]{2,1,0:T(8,128)(2,1)}, u32[]{:S(2)}) copy-start(bf16[2,64,512]{2,1,0:T(8,128)(2,1)} %get-tuple-element.151) | copy-start | bytes 393220 | tf_op jit(solution)/shard_map/while
  0.7 6.4 %collective-permute-start = (bf16[64,128]{1,0:T(8,128)(2,1)S(1)}, bf16[64,128]{1,0:T(8,128)(2,1)S(1)}, u32[]{:S(2)}, u32[]{:S(2)}) collective-permute-start(bf16[64,128]{1,0:T(8,128)(2,1)S(1)} %get-tuple-element.145), channel_id=1, source_target_pairs={{0,16},{1,17},{2,18},{3,19},{4,20},{5,21},{6,22},{7,23},{8,24},{9,... | collective-permute-start | bytes 49160 | tf_op jit(solution)/shard_map/while/body/eval_jaxpr/ppermute | solution.py:33
  38.5 36.4 %copy-start = (bf16[2,64,512]{2,1,0:T(8,128)(2,1)S(1)}, bf16[2,64,512]{2,1,0:T(8,128)(2,1)}, u32[]{:S(2)}) copy-start(bf16[2,64,512]{2,1,0:T(8,128)(2,1)} %get-tuple-element.151) | copy-start | bytes 393220 | tf_op jit(solution)/shard_map/while
  38.5 5.8 %collective-permute-start = (bf16[64,128]{1,0:T(8,128)(2,1)S(1)}, bf16[64,128]{1,0:T(8,128)(2,1)S(1)}, u32[]{:S(2)}, u32[]{:S(2)}) collective-permute-start(bf16[64,128]{1,0:T(8,128)(2,1)S(1)} %get-tuple-element.145), channel_id=1, source_target_pairs={{0,16},{1,17},{2,18},{3,19},{4,20},{5,21},{6,22},{7,23},{8,24},{9,... | collective-permute-start | bytes 49160 | tf_op jit(solution)/shard_map/while/body/eval_jaxpr/ppermute | solution.py:33
  75.4 3.8 %collective-permute-start.2 = (bf16[1,64,128]{2,1,0:T(8,128)(2,1)S(1)}, bf16[1,64,128]{2,1,0:T(8,128)(2,1)S(1)}, u32[]{:S(2)}, u32[]{:S(2)}) collective-permute-start(bf16[1,64,128]{2,1,0:T(8,128)(2,1)S(1)} %bitcast.58), channel_id=1, source_target_pairs={{0,2},{2,0},{4,6},{6,4},{8,10},{10,8},{12,14},{14,12},{1,3},{3,1},... | collective-permute-start | bytes 49160 | tf_op jit(solution)/shard_map/ppermute | solution.py:17
  79.1 4.0 %collective-permute-start.3 = (bf16[2,64,128]{2,1,0:T(8,128)(2,1)S(1)}, bf16[2,64,128]{2,1,0:T(8,128)(2,1)S(1)}, u32[]{:S(2)}, u32[]{:S(2)}) collective-permute-start(bf16[2,64,128]{2,1,0:T(8,128)(2,1)S(1)} %pad_maximum_fusion.2), channel_id=1, source_target_pairs={{0,4},{2,6},{4,0},{6,2},{8,12},{10,14},{12,8},{14,10},{1,5},{3,7},... | collective-permute-start | bytes 98312 | tf_op jit(solution)/shard_map/ppermute | solution.py:17
  83.2 5.7 %collective-permute-start.4 = (bf16[4,64,128]{2,1,0:T(8,128)(2,1)S(1)}, bf16[4,64,128]{2,1,0:T(8,128)(2,1)S(1)}, u32[]{:S(2)}, u32[]{:S(2)}) collective-permute-start(bf16[4,64,128]{2,1,0:T(8,128)(2,1)S(1)} %pad_maximum_fusion.1), channel_id=1, source_target_pairs={{0,8},{2,10},{4,12},{6,14},{8,0},{10,2},{12,4},{14,6},{1,9},{3,11}... | collective-permute-start | bytes 196616 | tf_op jit(solution)/shard_map/ppermute | solution.py:17
  88.9 0.9 copy-start.2
  90.1 0.9 copy-start.1
  91.0 5.6 %collective-permute-start.1 = (bf16[64,128]{1,0:T(8,128)(2,1)S(1)}, bf16[64,128]{1,0:T(8,128)(2,1)S(1)}, u32[]{:S(2)}, u32[]{:S(2)}) collective-permute-start(bf16[64,128]{1,0:T(8,128)(2,1)S(1)} %get-tuple-element.160), channel_id=1, source_target_pairs={{16,0},{17,1},{18,2},{19,3},{20,4},{21,5},{22,6},{23,7},{24,8},{25... | collective-permute-start | bytes 49160 | tf_op jit(solution)/shard_map/while/body/eval_jaxpr/ppermute | solution.py:33
  127.7 5.6 %collective-permute-start.1 = (bf16[64,128]{1,0:T(8,128)(2,1)S(1)}, bf16[64,128]{1,0:T(8,128)(2,1)S(1)}, u32[]{:S(2)}, u32[]{:S(2)}) collective-permute-start(bf16[64,128]{1,0:T(8,128)(2,1)S(1)} %get-tuple-element.160), channel_id=1, source_target_pairs={{16,0},{17,1},{18,2},{19,3},{20,4},{21,5},{22,6},{23,7},{24,8},{25... | collective-permute-start | bytes 49160 | tf_op jit(solution)/shard_map/while/body/eval_jaxpr/ppermute | solution.py:33
  164.3 0.6 copy-start.3
